TPU v7x, 256 devices: a whole 4x4x8 slice. The times are simulated.
256 devices in a mesh: gx: 64 (over x, z, core), af: 4 (over y).
Axes of the slice: x: 4, y: 4, z: 8, core: 2. Of those that a mesh axis runs over, the one named last changes fastest.
Arguments:
- scalar_field: float32 [128, 512, 512], P('gx', 'af'), may hold values from -256 to 256
- plane_sketch: float32 [128, 2, 256], P('gx'), may hold values from -0.5 to 0.5
- second_sketch: float32 [512, 256], P('af'), may hold values from -0.25 to 0.25
- third_sketch: float32 [512, 256], replicated, may hold values from -0.25 to 0.25
- mixing: float32 [2, 256, 128], replicated, may hold values from -0.375 to 0.375
- plane_targets: int32 [128, 2], replicated, may hold values from 0 to 7
- plane_signs: int32 [128, 2], replicated, may hold values from 0 to 1
Outputs:
- factor_second: float32 [512, 128], P(('af', 'gx'))
- factor_third: float32 [512, 128], P(('gx', 'af'))
- core_sketch: float32 [128, 128, 128], P('gx', 'af')
Inputs may be any that keep to these rules, and one draw needn't show every extreme that they name: `plane_targets`: block id of each of a plane's two entries in the core sketch; the two may coincide. `plane_signs`: 1 stands for a plus sign, 0 for a minus sign.
All inputs are finite; a program needn't handle non-finite values.
Results may differ from a plain program's by a relative error of at most 0.0003.
Values sent between devices are 32-bit elements; how exact they have to be, the bound alone decides.
A program may use at most 64 MiB of HBM per device.

v0:
```python
import jax
import jax.numpy as jnp
from jax import lax
from jax.sharding import PartitionSpec as P

BLOCK = 16
BLOCKS = 8
precise = lax.Precision.HIGHEST


def gram_of(ranged):
    return jnp.dot(ranged.T, ranged, precision=precise)


def orthonormal_rows(ranged, gram_matrix):
    lower_factor = jnp.linalg.cholesky(gram_matrix)
    return jax.scipy.linalg.solve_triangular(lower_factor, ranged.T, lower=True).T


def selector(targets, sign_values, row_count):
    row_ids = jnp.arange(row_count, dtype=jnp.int32)
    return jnp.sum(
        jnp.where(targets[None, :, :] == row_ids[:, None, None], sign_values[None, :, :], 0.0),
        axis=2,
    )


def body(
    scalar_field, plane_sketch, second_sketch, third_sketch, mixing, plane_targets, plane_signs
):
    planes, rows, cells = scalar_field.shape
    rank_cols = mixing.shape[2]
    gx_index = lax.axis_index("gx")
    af_index = lax.axis_index("af")
    gx_size = lax.axis_size("gx")
    af_size = lax.axis_size("af")
    along_second = jnp.einsum("pjl,lk->pjk", scalar_field, third_sketch, precision=precise)
    partial_second = jnp.einsum(
        "pjk,pk->jk", along_second, plane_sketch[:, 0, :], precision=precise
    )
    along_third = jnp.einsum("pjl,jk->plk", scalar_field, second_sketch, precision=precise)
    partial_third = jnp.einsum("plk,pk->lk", along_third, plane_sketch[:, 1, :], precision=precise)
    range_second_block = jnp.dot(partial_second, mixing[0], precision=precise)
    range_third = jnp.dot(partial_third, mixing[1], precision=precise)
    full_rows = rows * af_size
    range_second = lax.dynamic_update_slice_in_dim(
        jnp.zeros((full_rows, rank_cols), jnp.float32), range_second_block, af_index * rows, 0
    )
    both = lax.psum(jnp.stack([range_second, range_third]), ("gx", "af"))
    rows_second, rows_third = (both[0], both[1])
    factor_second_all = orthonormal_rows(rows_second, gram_of(rows_second))
    factor_third_all = orthonormal_rows(rows_third, gram_of(rows_third))
    out_second = full_rows // (gx_size * af_size)
    factor_second = lax.dynamic_slice_in_dim(
        factor_second_all, (af_index * gx_size + gx_index) * out_second, out_second, 0
    )
    factor_third = lax.dynamic_slice_in_dim(
        factor_third_all, (gx_index * af_size + af_index) * out_second, out_second, 0
    )
    basis_second = lax.dynamic_slice_in_dim(factor_second_all, af_index * rows, rows, 0)
    left_side = jnp.einsum("jr,pjl->prl", basis_second, scalar_field, precision=precise)
    projected = jnp.einsum("prl,ls->prs", left_side, factor_third_all, precision=precise)
    out_rows = BLOCKS * BLOCK // gx_size
    plane_ids = jnp.arange(plane_targets.shape[0], dtype=jnp.int32)
    all_targets = plane_targets * BLOCK + (plane_ids % BLOCK)[:, None]
    all_signs = (2 * plane_signs - 1).astype(jnp.float32)
    first_plane = gx_index * planes
    own_targets = lax.dynamic_slice_in_dim(all_targets, first_plane, planes, 0)
    own_signs = lax.dynamic_slice_in_dim(all_signs, first_plane, planes, 0)
    flattened = projected.reshape(planes, -1)
    select = selector(own_targets, own_signs, gx_size * out_rows)
    partial_core = lax.psum_scatter(
        jnp.dot(select, flattened, precision=precise).reshape(
            gx_size * out_rows, rank_cols, rank_cols
        ),
        "gx",
        scatter_dimension=0,
        tiled=True,
    )
    core_sketch = lax.psum_scatter(partial_core, "af", scatter_dimension=1, tiled=True)
    return (factor_second, factor_third, core_sketch)


def solution(mesh):
    in_specs = (P("gx", "af", None), P("gx", None, None), P("af", None), P(), P(), P(), P())
    out_specs = (P(("af", "gx"), None), P(("gx", "af"), None), P("gx", "af", None))
    return jax.shard_map(body, mesh=mesh, in_specs=in_specs, out_specs=out_specs, check_vma=False)
```

profile of v0, /device:TPU:2, one launch (start us, length us, event | category | flops | bytes accessed | tf_op | source)
XLA Modules:
  0.0 544.3 jit_solution(9497696338969925887)
XLA Ops:
  7.2 0.0 copy-start
  7.2 0.0 all-reduce.4.cloned.1.call-start
  7.2 0.8 fusion.37
  8.0 0.2 copy-done
  8.2 2.0 fusion.1
  10.2 1.5 convolution_bitcast_fusion.2
  11.7 1.6 fusion.3
  13.4 1.2 fusion.4
  14.6 0.8 pad_maximum_fusion
  15.4 0.0 all-reduce.4.cloned.1.call-update
  15.4 0.2 reduce-scatter.2.cloned.1.call-start
  15.7 0.7 add_convert_fusion
  16.4 0.7 multiply_add_fusion
  17.1 0.1 constant_dynamic-slice_fusion
  17.1 0.1 copy.38
  17.2 0.1 constant_dynamic-slice_fusion.1
  17.3 0.1 copy.37
  17.4 0.1 fusion.34
  17.5 253.1 %all-reduce.4.cloned.1.call-done = f32[2,512,128]{2,1,0:T(8,128)} async-done(((f32[2,512,128]{2,1,0:T(8,128)}), f32[2,512,128]{2,1,0:T(8,128)}) %all-reduce.4.cloned.1.call-update) | async-done | bytes 524304 | tf_op jit(solution)/shard_map/psum | solution.py:49
  270.6 1.6 fusion.13
  272.2 0.1 copy.35
  272.3 11.7 %cholesky.44 = f32[128,128]{1,0:T(8,128)S(1)} custom-call(f32[128,128]{1,0:T(8,128)S(1)} %fusion.32), custom_call_target="Cholesky" | custom-call | tf_op jit(solution)/shard_map/jit(cholesky)/cholesky | solution.py:16
  284.0 0.6 compare_reduce_fusion.1
  284.7 0.7 fusion.26
  285.4 9.8 %custom-call.6 = f32[1,128,128]{1,2,0:T(8,128)S(1)} custom-call(f32[1,128,128]{2,1,0:T(8,128)S(1)} %fusion.26), custom_call_target="InvertDiagBlocksLowerTriangular" | custom-call | tf_op jit(solution)/shard_map/jit(_solve_triangular)/triangular_solve | solution.py:17
  295.2 1.6 fusion.11
  296.8 0.1 copy.36
  296.9 11.7 %cholesky.55 = f32[128,128]{1,0:T(8,128)S(1)} custom-call(f32[128,128]{1,0:T(8,128)S(1)} %fusion.30), custom_call_target="Cholesky" | custom-call | tf_op jit(solution)/shard_map/jit(cholesky)/cholesky | solution.py:16
  308.7 0.6 compare_reduce_fusion
  309.3 0.7 fusion.27
  310.0 10.0 %custom-call.7 = f32[1,128,128]{1,2,0:T(8,128)S(1)} custom-call(f32[1,128,128]{2,1,0:T(8,128)S(1)} %fusion.27), custom_call_target="InvertDiagBlocksLowerTriangular" | custom-call | tf_op jit(solution)/shard_map/jit(_solve_triangular)/triangular_solve | solution.py:17
  320.0 1.4 fusion.8
  321.3 0.6 convolution_bitcast_fusion.1
  321.9 1.4 fusion.6
  323.3 0.6 convolution_bitcast_fusion.4
  323.9 6.8 %fusion.19 = f32[128,128,128]{2,0,1:T(8,128)S(1)} fusion(f32[1,2,128,128]{3,2,1,0:T(8,128)S(1)} %convolution_bitcast_fusion.4, f32[128,2]{0,1:T(2,128)S(1)} %fusion.34), kind=kOutput, calls=%fused_computation.27 | convolution fusion | flops 50331648 | bytes 8520704 | tf_op jit(solution)/shard_map/dot_general | solution.py:73
  330.7 8.3 %copy.39 = f32[128,128,128]{2,1,0:T(8,128)} copy(f32[128,128,128]{2,0,1:T(8,128)S(1)} %fusion.19) | data formatting | bytes 16777216 | tf_op jit(solution)/shard_map/dot_general | solution.py:73
  339.0 0.0 copy-start.1
  339.0 0.0 reduce-scatter.2.cloned.1.call-update
  339.0 0.0 all-reduce.6.cloned.1.call-start
  339.1 0.6 copy-done.1
  339.7 0.6 dynamic-slice.12
  340.9 147.6 %reduce-scatter.2.cloned.1.call-done = f32[2,128,128]{2,1,0:T(8,128)} async-done(((f32[128,128,128]{2,1,0:T(8,128)}), f32[2,128,128]{2,1,0:T(8,128)}) %reduce-scatter.2.cloned.1.call-update) | async-done | bytes 131088 | tf_op jit(solution)/shard_map/reduce_scatter | solution.py:72
  488.6 1.6 copy.40
  490.2 0.0 all-reduce.6.cloned.1.call-update
  490.2 0.1 dynamic-slice_bitcast_fusion.1
  490.3 0.6 copy.41
  490.9 0.1 dynamic-slice_bitcast_fusion
  491.0 0.6 copy.42
  491.7 44.7 %all-reduce.6.cloned.1.call-done = f32[2,128,128]{2,0,1:T(2,128)} async-done(((f32[2,128,128]{2,0,1:T(2,128)}), f32[2,128,128]{2,0,1:T(2,128)}) %all-reduce.6.cloned.1.call-update) | async-done | bytes 131088
  536.4 0.8 constant_dynamic-slice_fusion.2
  537.1 0.6 copy.43
  (7 shorter events, 0.1 us)
Async XLA Ops:
  7.2 1.1 copy-start
  7.2 263.4 %all-reduce.4.cloned.1.call-start = ((), (), s32[]{:S(2)}) async-start(), calls=%async_computation.1 | async-start | bytes 1048576 | tf_op jit(solution)/shard_map/psum | solution.py:49
  15.4 473.1 %reduce-scatter.2.cloned.1.call-start = ((), (), s32[]{:S(2)}) async-start(), calls=%async_computation.2 | async-start | bytes 8519680 | tf_op jit(solution)/shard_map/reduce_scatter | solution.py:72
  339.0 0.7 copy-start.1
  339.0 197.4 %all-reduce.6.cloned.1.call-start = ((), (), s32[]{:S(2)}) async-start(), calls=%async_computation.3 | async-start | bytes 262144
Sparse Core Ops, SparseCore 0:
  15.6 254.9 all-reduce.3
  339.1 149.3 reduce-scatter.1
  491.0 45.3 all-reduce.5
where the time goes:
time: 545 us; the launch traced here: 544 us
  waiting for transfers between devices  445 us (82%)
  other arithmetic  48.2 us (9%)
  matrix products  20.2 us (4%)
  local copies, waits for them, and re-layouts  15.5 us (3%)
  between operations  14.6 us (3%)
    psum x1, waiting for transfers between devices, body(): both = lax.psum(jnp.stack([range_second, range_third]), ('gx', 'af'))  253 us
    reduce_scatter x1, waiting for transfers between devices, body(): lax.psum_scatter(jnp.dot(select, flattened, precision=precise).reshape(gx...  148 us
    unnamed x4, waiting for transfers between devices  44.8 us
    another operation x6, other arithmetic, orthonormal_rows(): lower_factor = jnp.linalg.cholesky(gram_matrix)  24.8 us
    another operation x4, other arithmetic, orthonormal_rows(): jax.scipy.linalg.solve_triangular(lower_factor, ranged.T, lower=True)  21.1 us
  transfers between devices with their start and end apart: 3, of which 3 were waited for; matrix products, arithmetic and copies ran while one was open for 1% of the time, Pallas kernels for 0%

commit v1 on v0

--- a/solution.py
+++ b/solution.py
@@ -46,7 +46,7 @@
     range_second = lax.dynamic_update_slice_in_dim(
         jnp.zeros((full_rows, rank_cols), jnp.float32), range_second_block, af_index * rows, 0
     )
-    both = lax.psum(jnp.stack([range_second, range_third]), ("gx", "af"))
+    both = lax.psum(lax.psum(jnp.stack([range_second, range_third]), "af"), "gx")
     rows_second, rows_third = (both[0], both[1])
     factor_second_all = orthonormal_rows(rows_second, gram_of(rows_second))
     factor_third_all = orthonormal_rows(rows_third, gram_of(rows_third))

time: 545 us -> 524 us (0.961)
  waiting for transfers between devices: 445 us -> 425 us
    psum x1 -> x2, waiting for transfers between devices: 253 us -> 234 us  [the longest x1 185 us: body(): lax.psum(lax.psum(jnp.stack([range_second, range_third]), 'af'), 'gx')]
    unnamed x4 -> x5, waiting for transfers between devices: 44.8 us -> 44.6 us
  transfers between devices with their start and end apart: 3 -> 4, of which waited for: 3 -> 4; matrix products, arithmetic and copies ran while one was open for 1% -> 1% of each run, Pallas kernels for 0% -> 0%
where the time goes in v1:
time: 524 us
  waiting for transfers between devices  425 us (81%)
  other arithmetic  48.2 us (9%)
  matrix products  20.2 us (4%)
  local copies, waits for them, and re-layouts  15.5 us (3%)
  between operations  14.6 us (3%)
    psum x1, waiting for transfers between devices, body(): lax.psum(lax.psum(jnp.stack([range_second, range_third]), 'af'), 'gx')  185 us
    reduce_scatter x1, waiting for transfers between devices, body(): lax.psum_scatter(jnp.dot(select, flattened, precision=precise).reshape(gx...  146 us
    psum x1, waiting for transfers between devices, body(): lax.psum(jnp.stack([range_second, range_third]), 'af')  49.8 us
    unnamed x5, waiting for transfers between devices  44.6 us
    another operation x6, other arithmetic, orthonormal_rows(): lower_factor = jnp.linalg.cholesky(gram_matrix)  24.8 us
    another operation x4, other arithmetic, orthonormal_rows(): jax.scipy.linalg.solve_triangular(lower_factor, ranged.T, lower=True)  21.1 us
  transfers between devices with their start and end apart: 4, of which 4 were waited for; matrix products, arithmetic and copies ran while one was open for 1% of the time, Pallas kernels for 0%

profile of v1, /device:TPU:2, one launch (start us, length us, event | category | flops | bytes accessed | tf_op | source)
XLA Modules:
  0.0 523.7 jit_solution(240091031834976698)
XLA Ops:
  7.2 0.0 copy-start
  7.2 0.0 all-reduce.5.cloned.1.call-start
  7.2 0.8 fusion.37
  8.0 0.2 copy-done
  8.2 2.0 fusion.1
  10.2 1.5 convolution_bitcast_fusion.2
  11.7 1.6 fusion.3
  13.4 1.2 fusion.4
  14.6 0.8 pad_maximum_fusion
  15.4 0.0 all-reduce.5.cloned.1.call-update
  15.4 0.0 all-reduce.7.cloned.1.call-start
  15.5 0.7 add_convert_fusion
  16.2 0.7 multiply_add_fusion
  16.9 49.8 %all-reduce.5.cloned.1.call-done = f32[2,512,128]{2,1,0:T(8,128)} async-done(((f32[2,512,128]{2,1,0:T(8,128)}), f32[2,512,128]{2,1,0:T(8,128)}) %all-reduce.5.cloned.1.call-update) | async-done | bytes 524304 | tf_op jit(solution)/shard_map/psum | solution.py:49
  66.7 0.0 all-reduce.7.cloned.1.call-update
  66.7 0.2 reduce-scatter.2.cloned.1.call-start
  66.9 0.1 constant_dynamic-slice_fusion
  67.0 0.1 copy.38
  67.1 0.1 constant_dynamic-slice_fusion.1
  67.2 0.1 copy.37
  67.3 0.1 fusion.34
  67.4 184.5 %all-reduce.7.cloned.1.call-done = f32[2,512,128]{2,1,0:T(8,128)} async-done(((f32[2,512,128]{2,1,0:T(8,128)}), f32[2,512,128]{2,1,0:T(8,128)}) %all-reduce.7.cloned.1.call-update) | async-done | bytes 524304 | tf_op jit(solution)/shard_map/psum | solution.py:49
  251.9 1.6 fusion.13
  253.5 0.1 copy.35
  253.7 11.7 %cholesky.44 = f32[128,128]{1,0:T(8,128)S(1)} custom-call(f32[128,128]{1,0:T(8,128)S(1)} %fusion.32), custom_call_target="Cholesky" | custom-call | tf_op jit(solution)/shard_map/jit(cholesky)/cholesky | solution.py:16
  265.4 0.6 compare_reduce_fusion.1
  266.0 0.7 fusion.26
  266.7 9.8 %custom-call.6 = f32[1,128,128]{1,2,0:T(8,128)S(1)} custom-call(f32[1,128,128]{2,1,0:T(8,128)S(1)} %fusion.26), custom_call_target="InvertDiagBlocksLowerTriangular" | custom-call | tf_op jit(solution)/shard_map/jit(_solve_triangular)/triangular_solve | solution.py:17
  276.5 1.6 fusion.11
  278.1 0.1 copy.36
  278.3 11.7 %cholesky.55 = f32[128,128]{1,0:T(8,128)S(1)} custom-call(f32[128,128]{1,0:T(8,128)S(1)} %fusion.30), custom_call_target="Cholesky" | custom-call | tf_op jit(solution)/shard_map/jit(cholesky)/cholesky | solution.py:16
  290.0 0.6 compare_reduce_fusion
  290.7 0.7 fusion.27
  291.3 10.0 %custom-call.7 = f32[1,128,128]{1,2,0:T(8,128)S(1)} custom-call(f32[1,128,128]{2,1,0:T(8,128)S(1)} %fusion.27), custom_call_target="InvertDiagBlocksLowerTriangular" | custom-call | tf_op jit(solution)/shard_map/jit(_solve_triangular)/triangular_solve | solution.py:17
  301.3 1.4 fusion.8
  302.7 0.6 convolution_bitcast_fusion.1
  303.3 1.4 fusion.6
  304.6 0.6 convolution_bitcast_fusion.4
  305.2 6.8 %fusion.19 = f32[128,128,128]{2,0,1:T(8,128)S(1)} fusion(f32[1,2,128,128]{3,2,1,0:T(8,128)S(1)} %convolution_bitcast_fusion.4, f32[128,2]{0,1:T(2,128)S(1)} %fusion.34), kind=kOutput, calls=%fused_computation.27 | convolution fusion | flops 50331648 | bytes 8520704 | tf_op jit(solution)/shard_map/dot_general | solution.py:73
  312.0 8.3 %copy.39 = f32[128,128,128]{2,1,0:T(8,128)} copy(f32[128,128,128]{2,0,1:T(8,128)S(1)} %fusion.19) | data formatting | bytes 16777216 | tf_op jit(solution)/shard_map/dot_general | solution.py:73
  320.3 0.0 copy-start.1
  320.3 0.0 reduce-scatter.2.cloned.1.call-update
  320.4 0.0 all-reduce.9.cloned.1.call-start
  320.4 0.6 copy-done.1
  321.0 0.6 dynamic-slice.12
  322.3 145.9 %reduce-scatter.2.cloned.1.call-done = f32[2,128,128]{2,1,0:T(8,128)} async-done(((f32[128,128,128]{2,1,0:T(8,128)}), f32[2,128,128]{2,1,0:T(8,128)}) %reduce-scatter.2.cloned.1.call-update) | async-done | bytes 131088 | tf_op jit(solution)/shard_map/reduce_scatter | solution.py:72
  468.1 1.6 copy.40
  469.8 0.0 all-reduce.9.cloned.1.call-update
  469.8 0.1 dynamic-slice_bitcast_fusion.1
  469.9 0.6 copy.41
  470.6 0.1 dynamic-slice_bitcast_fusion
  470.6 0.6 copy.42
  471.3 44.5 %all-reduce.9.cloned.1.call-done = f32[2,128,128]{2,0,1:T(2,128)} async-done(((f32[2,128,128]{2,0,1:T(2,128)}), f32[2,128,128]{2,0,1:T(2,128)}) %all-reduce.9.cloned.1.call-update) | async-done | bytes 131088
  515.8 0.8 constant_dynamic-slice_fusion.2
  516.6 0.6 copy.43
  (7 shorter events, 0.1 us)
Async XLA Ops:
  7.2 1.1 copy-start
  7.2 59.5 %all-reduce.5.cloned.1.call-start = ((), (), s32[]{:S(2)}) async-start(), calls=%async_computation.1 | async-start | bytes 1048576 | tf_op jit(solution)/shard_map/psum | solution.py:49
  15.4 236.5 %all-reduce.7.cloned.1.call-start = ((), (), s32[]{:S(2)}) async-start(), calls=%async_computation.2 | async-start | bytes 1048576 | tf_op jit(solution)/shard_map/psum | solution.py:49
  66.7 401.4 %reduce-scatter.2.cloned.1.call-start = ((), (), s32[]{:S(2)}) async-start(), calls=%async_computation.3 | async-start | bytes 8519680 | tf_op jit(solution)/shard_map/reduce_scatter | solution.py:72
  320.3 0.7 copy-start.1
  320.4 195.5 %all-reduce.9.cloned.1.call-start = ((), (), s32[]{:S(2)}) async-start(), calls=%async_computation.4 | async-start | bytes 262144
Sparse Core Ops, SparseCore 0:
  15.6 51.0 all-reduce.4
  70.2 181.6 all-reduce.6
  320.5 147.6 reduce-scatter.1
  470.4 45.3 all-reduce.8
